TPU v7x, 32 devices: a whole 2x2x4 slice. The times are simulated.
32 devices in a mesh: groups: 1, seq: 32 (over z, y, x, core).
Axes of the slice: x: 2, y: 2, z: 4, core: 2. Of those that a mesh axis runs over, the one named last changes fastest.
Arguments:
- q_gate: bfloat16 [4096, 4096], P(('groups', 'seq')), may hold values from -6 to 6
- values_in: bfloat16 [4096, 4096], P(('groups', 'seq')), may hold values from -6 to 6
- decay_rate: float32 [4096, 16], replicated, as said below
- residue: float32 [4096, 16], replicated, may hold values from -3 to 3
- skip_gain: float32 [4096], replicated, may hold values from 0.5 to 1.5
- out_weight: bfloat16 [4096, 2048], P('seq'), may hold values from -0.09375 to 0.09375
Outputs:
- mixed: bfloat16 [4096, 2048], P(('groups', 'seq'))
Inputs may be any that keep to these rules, and one draw needn't show every extreme that they name: `decay_rate`: every rate is positive and at most about 1/30.
All inputs are finite; a program needn't handle non-finite values.
Results may differ from a plain program's by a relative error of at most 0.0052.
Values may be sent and summed in bfloat16 or wider, within the bound.
A program may use at most 256 MiB of HBM per device.

v0:
```python
import jax
import jax.numpy as jnp
from jax import lax
from jax.sharding import PartitionSpec as P

ORDER = 16
BLOCK = 32


def entering(value, axis, join, neutral):
    count, mine = (lax.axis_size(axis), lax.axis_index(axis))
    pieces = jax.tree.map(lambda part: lax.all_gather(part, axis), value)
    running = jax.tree.map(
        lambda part, zero: jnp.full_like(part, 0) + jnp.asarray(zero, part.dtype), value, neutral
    )

    def hop(position, running):
        longer = join(running, jax.tree.map(lambda part: part[position], pieces))
        return jax.tree.map(lambda new, old: jnp.where(position < mine, new, old), longer, running)

    return lax.fori_loop(0, count - 1, hop, running)


def on_device(q_gate, values_in, decay_rate, residue, skip_gain, out_weight):
    tok_rows = q_gate.shape[0]
    width = q_gate.shape[1]
    block_count = tok_rows // BLOCK
    rate_modes = decay_rate.T
    mode_scale = jnp.sqrt(-jnp.expm1(-2.0 * rate_modes))
    mode_coef = residue.T * mode_scale
    position = jnp.arange(BLOCK, dtype=jnp.float32)
    tap_values = jnp.sum(
        mode_coef[None] * jnp.exp(-position[:, None, None] * rate_modes[None]), axis=1
    )
    tap_round = tap_values.astype(jnp.bfloat16)
    offsets = jnp.arange(BLOCK)[:, None] - jnp.arange(BLOCK)[None, :]
    selector = (
        (jnp.arange(BLOCK)[:, None, None] == offsets[None])
        .astype(jnp.bfloat16)
        .reshape(BLOCK, BLOCK * BLOCK)
    )
    toeplitz = jnp.dot(tap_round.T, selector, preferred_element_type=jnp.bfloat16).reshape(
        width, BLOCK, BLOCK
    )
    blocked = values_in.reshape(block_count, BLOCK, width)
    local_part = jnp.einsum("dts,nsd->ntd", toeplitz, blocked, preferred_element_type=jnp.float32)
    blocked_wide = blocked.astype(jnp.float32)
    end_weight = jnp.exp(-(BLOCK - 1 - position)[:, None, None] * rate_modes[None])
    block_ends = jnp.einsum(
        "tkd,ntd->nkd", end_weight, blocked_wide, precision=lax.Precision.HIGHEST
    )
    step_decay = jnp.exp(-BLOCK * rate_modes)

    def advance(carry_state, inflow):
        return (step_decay * carry_state + inflow, carry_state)

    end_state, starts_local = lax.scan(advance, jnp.zeros((ORDER, width), jnp.float32), block_ends)
    shard_decay = jnp.exp(-tok_rows * rate_modes)

    def combine_pairs(earlier, later):
        return (earlier[0] * later[0], earlier[1] * later[0] + later[1])

    identity = (jnp.ones_like(shard_decay), jnp.zeros_like(end_state))
    scanned = entering((shard_decay, end_state), "seq", combine_pairs, identity)
    incoming = scanned[1]
    block_index = jnp.arange(block_count, dtype=jnp.float32)
    starts = (
        starts_local
        + jnp.exp(-(BLOCK * block_index)[:, None, None] * rate_modes[None]) * incoming[None]
    )
    reach_table = mode_coef[None] * jnp.exp(-(position + 1.0)[:, None, None] * rate_modes[None])
    correction = jnp.einsum("tkd,nkd->ntd", reach_table, starts, precision=lax.Precision.HIGHEST)
    conv = (local_part + correction).reshape(tok_rows, width)
    gated = (
        q_gate.astype(jnp.float32) * (conv + skip_gain[None] * values_in.astype(jnp.float32))
    ).astype(jnp.bfloat16)
    weights = lax.all_gather(out_weight, "seq", axis=0, tiled=True)
    mixed = jnp.dot(gated, weights, preferred_element_type=jnp.float32)
    return mixed.astype(jnp.bfloat16)


def solution(mesh):
    in_specs = (
        P(("groups", "seq"), None),
        P(("groups", "seq"), None),
        P(),
        P(),
        P(),
        P("seq", None),
    )
    out_specs = P(("groups", "seq"), None)
    return jax.shard_map(
        on_device, mesh=mesh, in_specs=in_specs, out_specs=out_specs, check_vma=False
    )
```

profile of v0, /device:TPU:0, one launch (start us, length us, event | category | flops | bytes accessed | tf_op | source)
XLA Modules:
  0.0 299.8 jit_solution(8403443552745695005)
XLA Ops:
  6.5 1.9 multiply_exponential_fusion
  8.6 1.5 copy.31
  10.1 6.2 %copy.34 = bf16[4,32,4096]{1,0,2:T(4,128)(2,1)} copy(bf16[4,32,4096]{2,1,0:T(8,128)(2,1)} %bitcast.53) | data formatting | bytes 2097152 | tf_op jit(solution)/shard_map/reshape | solution.py:45
  16.3 34.1 %fusion.13 = f32[4,16,4096]{1,0,2:T(4,128)} fusion(bf16[4,32,4096]{1,0,2:T(4,128)(2,1)} %copy.34, f32[32]{0:T(128)S(1)} %subtract_negate_fusion, f32[16,4096]{0,1:T(8,128)S(1)} %copy.31), kind=kOutput, calls=%fused_computation.19 | convolution fusion | flops 102760448 | bytes 2359424 | tf_op jit(solution)/shard_map/tkd,ntd->nkd/dot_general | solution.py:49
  50.4 7.5 %copy.36 = f32[4,16,4096]{2,1,0:T(8,128)} copy(f32[4,16,4096]{1,0,2:T(4,128)} %fusion.13) | data formatting | bytes 2097152
  57.9 7.5 %while.27 = (s32[]{:T(128)}, f32[16,4096]{1,0:T(8,128)S(1)}, f32[4,16,4096]{2,1,0:T(8,128)}, f32[16,4096]{1,0:T(8,128)S(1)}, f32[4,16,4096]{2,1,0:T(8,128)}, /*index=5*/s32[]{:T(128)}, s32[]{:T(128)}) while((s32[]{:T(128)}, f32[16,4096]{1,0:T(8,128)S(1)}, f32[4,16,4096]{2,1,0:T(8,128)}, f32[16,4096]{1,0:T(8,128)S(1)}, ...), condition=%wide.region_2.3_spmd.clone, body=%wide.region_1.2_spmd.clone.sunk | while | flops 262147 | bytes 1572968 | solution.py:57
  67.0 2.0 copy.30
  68.9 25.7 %multiply_reduce_fusion = bf16[32,4096]{0,1:T(8,128)(2,1)} fusion(f32[16,4096]{0,1:T(8,128)S(1)} %copy.31, f32[32]{0:T(128)S(1)} %iota_negate_fusion, f32[16,4096]{0,1:T(8,128)} %copy.30), kind=kLoop, calls=%fused_computation.12 | loop fusion | flops 6160384 | bytes 786560 | tf_op jit(solution)/shard_map/reduce_sum | solution.py:32
  94.6 1.5 copy.32
  96.2 5.6 %fusion.20 = bf16[4096,32,32]{0,2,1:T(8,128)(2,1)} fusion(s32[32,32]{1,0:T(8,128)S(1)} %iota_subtract_fusion, bf16[32,4096]{1,0:T(8,128)(2,1)S(1)} %copy.32), kind=kOutput, calls=%fused_computation.26 | convolution fusion | flops 268468224 | bytes 8654848 | tf_op jit(solution)/shard_map/dot_general | solution.py:42
  101.7 44.1 %copy.33 = bf16[4096,32,32]{2,1,0:T(8,128)(2,1)} copy(bf16[4096,32,32]{0,2,1:T(8,128)(2,1)} %fusion.20) | data formatting | bytes 16777216 | tf_op jit(solution)/shard_map/dot_general | solution.py:42
  145.9 22.9 %fusion.24 = f32[4096,32,4]{1,2,0:T(4,128)} fusion(bf16[4096,32,32]{2,1,0:T(8,128)(2,1)} %copy.33, bf16[4,32,4096]{1,0,2:T(4,128)(2,1)} %copy.34), kind=kOutput, calls=%fused_computation.38 | convolution fusion | flops 33554432 | bytes 11534336 | tf_op jit(solution)/shard_map/dts,nsd->ntd/dot_general | solution.py:46
  168.8 39.5 %while.28 = (s32[]{:T(128)}, f32[16,4096]{1,0:T(8,128)S(1)}, s32[]{:T(128)}, f32[32,16,4096]{2,1,0:T(8,128)}, f32[32,16,4096]{2,1,0:T(8,128)}, /*index=5*/s32[]{:T(128)}, s32[]{:T(128)}) while((s32[]{:T(128)}, f32[16,4096]{1,0:T(8,128)S(1)}, s32[]{:T(128)}, f32[32,16,4096]{2,1,0:T(8,128)}, f32[32,16,4096]{2,1,0:T(8,128)}, ...), condition=%wide.region_4.5_spmd.clone, body=%wide.region_3.4_spmd.clone.sunk | while | flops 262148 | bytes 1048685 | solution.py:21
  177.7 1.3 fusion.35
  179.0 1.3 fusion.35
  190.5 1.3 fusion.35
  199.4 1.3 fusion.35
  208.3 2.5 multiply_add_fusion
  210.9 6.9 %copy.37 = f32[4,16,4096]{1,0,2:T(4,128)} copy(f32[4,16,4096]{2,1,0:T(8,128)} %multiply_add_fusion) | data formatting | bytes 2097152 | tf_op jit(solution)/shard_map/add | solution.py:68
  217.7 47.3 %bitcast_add_fusion.2 = f32[4,32,4096]{1,0,2:T(4,128)} fusion(f32[4096,32,4]{1,2,0:T(4,128)} %fusion.24, f32[4,16,4096]{1,0,2:T(4,128)} %copy.37, f32[32]{0:T(128)S(1)} %add_negate_fusion, f32[16,4096]{0,1:T(8,128)S(1)} %copy.31, f32[16,4096]{0,1:T(8,128)} %copy.30), kind=kOutput, calls=%fused_computation.18 | convolution fusion | flops 105381888 | bytes 5767296 | tf_op jit(solution)/shard_map/tkd,nkd->ntd/dot_general | solution.py:72
  265.1 7.0 %copy.38 = f32[4,32,4096]{2,1,0:T(8,128)S(1)} copy(f32[4,32,4096]{1,0,2:T(4,128)} %bitcast_add_fusion.2) | data formatting | bytes 4194304 | tf_op jit(solution)/shard_map/add | solution.py:73
  272.1 2.2 fusion.19
  274.3 10.2 %all-gather.6.cloned.1.call-done = bf16[4096,2048]{1,0:T(8,128)(2,1)} async-done(((bf16[128,2048]{1,0:T(8,128)(2,1)}), bf16[4096,2048]{1,0:T(8,128)(2,1)}) %all-gather.6.cloned.1.call-update) | async-done | bytes 16777232 | tf_op jit(solution)/shard_map/all_gather | solution.py:77
  284.4 8.9 %convolution_convert_fusion = bf16[128,2048]{1,0:T(8,128)(2,1)} fusion(bf16[128,4096]{1,0:T(8,128)(2,1)S(1)} %fusion.19, bf16[4096,2048]{1,0:T(8,128)(2,1)} %all-gather.6.cloned.1.call-done), kind=kOutput, calls=%fused_computation.20 | convolution fusion | flops 2147745792 | bytes 18350080 | tf_op jit(solution)/shard_map/dot_general | solution.py:78
  (57 shorter events, 42.7 us)
Async XLA Ops:
  6.5 162.2 %all-gather.8.cloned.1.call-start = ((), (), s32[]{:S(2)}) async-start(), calls=%async_computation.1 | async-start | bytes 8650752 | tf_op jit(solution)/shard_map/all_gather | solution.py:12
  8.5 160.3 %all-gather.10.cloned.1.call-start = ((), (), s32[]{:S(2)}) async-start(), calls=%async_computation.2 | async-start | bytes 8650752 | tf_op jit(solution)/shard_map/all_gather | solution.py:12
  65.4 0.7 copy-start
  66.2 218.3 %all-gather.6.cloned.1.call-start = ((), (), s32[]{:S(2)}) async-start(), calls=%async_computation | async-start | bytes 17301504 | tf_op jit(solution)/shard_map/all_gather | solution.py:77
  145.9 62.4 %copy-start.1 = (f32[4096,16]{0,1:T(8,128)S(1)}, f32[4096,16]{0,1:T(8,128)}, u32[]{:S(2)}) copy-start(f32[4096,16]{0,1:T(8,128)} %param.12) | copy-start | bytes 786436
  265.1 7.0 %copy-start.2 = (f32[4096]{0:T(1024)S(1)}, f32[4096]{0:T(1024)}, u32[]{:S(2)}) copy-start(f32[4096]{0:T(1024)} %param.14) | copy-start | bytes 49156
Sparse Core Ops, SparseCore 0:
  10.2 79.7 all-gather.7
  92.9 75.6 all-gather.9
  171.4 112.9 all-gather.5
where the time goes:
time: 302 us; the launch traced here: 300 us
  matrix products  119 us (39%)
  other arithmetic  78.6 us (26%)
  local copies, waits for them, and re-layouts  77.5 us (26%)
  between operations  13.2 us (4%)
  waiting for transfers between devices  10.7 us (4%)
    dot_general x1, matrix products, on_device(): jnp.einsum('tkd,nkd->ntd', reach_table, starts, precision=lax.Precision.H...  47.3 us
    dot_general x1, local copies, waits for them, and re-layouts, on_device(): jnp.dot(tap_round.T, selector, preferred_element_type=jnp.bfloat16)  44.1 us
    select_n x31, other arithmetic, hop(): jnp.where(position < mine, new, old)  38.9 us
    dot_general x1, matrix products, on_device(): jnp.einsum('tkd,ntd->nkd', end_weight, blocked_wide, precision=lax.Precis...  34.1 us
    reduce_sum x1, other arithmetic, on_device(): jnp.sum(mode_coef[None] * jnp.exp(-position[:, None, None] * rate_modes[N...  25.7 us
    dot_general x1, matrix products, on_device(): jnp.einsum('dts,nsd->ntd', toeplitz, blocked, preferred_element_type=jnp....  22.9 us
    all_gather x1, waiting for transfers between devices, on_device(): weights = lax.all_gather(out_weight, 'seq', axis=0, tiled=True)  10.2 us
    dot_general x1, matrix products, on_device(): mixed = jnp.dot(gated, weights, preferred_element_type=jnp.float32)  8.9 us
  transfers between devices with their start and end apart: 3, of which 1 were waited for; matrix products, arithmetic and copies ran while one was open for 88% of the time, Pallas kernels for 0%

commit v1 on v0

--- a/solution.py
+++ b/solution.py
@@ -74,7 +74,9 @@
     gated = (
         q_gate.astype(jnp.float32) * (conv + skip_gain[None] * values_in.astype(jnp.float32))
     ).astype(jnp.bfloat16)
-    weights = lax.all_gather(out_weight, "seq", axis=0, tiled=True)
+    weights = jnp.concatenate(
+        lax.all_to_all(jnp.stack([out_weight] * lax.axis_size("seq")), "seq", 0, 0), axis=0
+    )
     mixed = jnp.dot(gated, weights, preferred_element_type=jnp.float32)
     return mixed.astype(jnp.bfloat16)
 

time: 302 us -> 511 us (1.69)
  waiting for transfers between devices: 10.7 us -> 206 us
  starting transfers between devices: 0.27 us -> 7.62 us
  local copies, waits for them, and re-layouts: 77.5 us -> 83.6 us
    all_gather x2, waiting for transfers between devices: 0.01 us -> 144 us  [entering(): pieces = jax.tree.map(lambda part: lax.all_gather(part, axis), value)]
    all_to_all x0 -> x1, waiting for transfers between devices: none -> 62.8 us  [on_device(): lax.all_to_all(jnp.stack([out_weight] * lax.axis_size('seq')), 'seq', 0, 0)]
    all_gather x1 -> x0, waiting for transfers between devices: 10.2 us -> none  [on_device(): weights = lax.all_gather(out_weight, 'seq', axis=0, tiled=True)]
    all_to_all x0 -> x1, starting transfers between devices: none -> 7.57 us  [on_device(): lax.all_to_all(jnp.stack([out_weight] * lax.axis_size('seq')), 'seq', 0, 0)]
    another operation x0 -> x1, local copies, waits for them, and re-layouts: none -> 6.04 us  [on_device(): jnp.stack([out_weight] * lax.axis_size('seq'))]
  transfers between devices with their start and end apart: 3 -> 3, of which waited for: 1 -> 2; matrix products, arithmetic and copies ran while one was open for 88% -> 53% of each run, Pallas kernels for 0% -> 0%
where the time goes in v1:
time: 511 us; the launch traced here: 509 us
  waiting for transfers between devices  206 us (40%)
  matrix products  119 us (23%)
  local copies, waits for them, and re-layouts  83.6 us (16%)
  other arithmetic  78.4 us (15%)
  between operations  13.5 us (3%)
  starting transfers between devices  7.62 us (1%)
    all_gather x2, waiting for transfers between devices, entering(): pieces = jax.tree.map(lambda part: lax.all_gather(part, axis), value)  144 us
    all_to_all x1, waiting for transfers between devices, on_device(): lax.all_to_all(jnp.stack([out_weight] * lax.axis_size('seq')), 'seq', 0, 0)  62.8 us
    dot_general x1, matrix products, on_device(): jnp.einsum('tkd,nkd->ntd', reach_table, starts, precision=lax.Precision.H...  47.3 us
    dot_general x1, local copies, waits for them, and re-layouts, on_device(): jnp.dot(tap_round.T, selector, preferred_element_type=jnp.bfloat16)  44.1 us
    select_n x31, other arithmetic, hop(): jnp.where(position < mine, new, old)  38.7 us
    dot_general x1, matrix products, on_device(): jnp.einsum('tkd,ntd->nkd', end_weight, blocked_wide, precision=lax.Precis...  34.1 us
    reduce_sum x1, other arithmetic, on_device(): jnp.sum(mode_coef[None] * jnp.exp(-position[:, None, None] * rate_modes[N...  25.7 us
    dot_general x1, matrix products, on_device(): jnp.einsum('dts,nsd->ntd', toeplitz, blocked, preferred_element_type=jnp....  22.7 us
  transfers between devices with their start and end apart: 3, of which 2 were waited for; matrix products, arithmetic and copies ran while one was open for 53% of the time, Pallas kernels for 0%

profile of v1, /device:TPU:0, one launch (start us, length us, event | category | flops | bytes accessed | tf_op | source)
XLA Modules:
  0.0 508.8 jit_solution(3938349166019980672)
XLA Ops:
  6.5 1.9 multiply_exponential_fusion
  8.6 1.5 copy.31
  10.1 6.2 %copy.34 = bf16[4,32,4096]{1,0,2:T(4,128)(2,1)} copy(bf16[4,32,4096]{2,1,0:T(8,128)(2,1)} %bitcast.54) | data formatting | bytes 2097152 | tf_op jit(solution)/shard_map/reshape | solution.py:45
  16.3 34.1 %fusion.13 = f32[4,16,4096]{1,0,2:T(4,128)} fusion(bf16[4,32,4096]{1,0,2:T(4,128)(2,1)} %copy.34, f32[32]{0:T(128)S(1)} %subtract_negate_fusion, f32[16,4096]{0,1:T(8,128)S(1)} %copy.31), kind=kOutput, calls=%fused_computation.19 | convolution fusion | flops 102760448 | bytes 2359424 | tf_op jit(solution)/shard_map/tkd,ntd->nkd/dot_general | solution.py:49
  50.4 7.6 %copy.36 = f32[4,16,4096]{2,1,0:T(8,128)} copy(f32[4,16,4096]{1,0,2:T(4,128)} %fusion.13) | data formatting | bytes 2097152
  58.0 7.5 %while.27 = (s32[]{:T(128)}, f32[16,4096]{1,0:T(8,128)S(1)}, f32[4,16,4096]{2,1,0:T(8,128)}, f32[16,4096]{1,0:T(8,128)S(1)}, f32[4,16,4096]{2,1,0:T(8,128)}, /*index=5*/s32[]{:T(128)}, s32[]{:T(128)}) while((s32[]{:T(128)}, f32[16,4096]{1,0:T(8,128)S(1)}, f32[4,16,4096]{2,1,0:T(8,128)}, f32[16,4096]{1,0:T(8,128)S(1)}, ...), condition=%wide.region_2.3_spmd.clone, body=%wide.region_1.2_spmd.clone.sunk | while | flops 262147 | bytes 1572968 | solution.py:57
  66.2 6.0 %stack.2 = bf16[32,128,2048]{2,1,0:T(8,128)(2,1)} broadcast(bf16[128,2048]{1,0:T(8,128)(2,1)S(1)} %copy-done.2), dimensions={1,2} | broadcast | bytes 17301504 | tf_op jit(solution)/shard_map/stack | solution.py:78
  72.3 7.6 %all-to-all-start = ((bf16[32,128,2048]{2,1,0:T(8,128)(2,1)}), bf16[32,128,2048]{2,1,0:T(8,128)(2,1)}, u32[]{:S(2)}, u32[]{:S(2)}) async-start(bf16[32,128,2048]{2,1,0:T(8,128)(2,1)} %stack.2), calls=%async_computation | async-start | bytes 33554432 | tf_op jit(solution)/shard_map/all_to_all | solution.py:78
  79.9 2.0 copy.30
  81.9 25.7 %multiply_reduce_fusion = bf16[32,4096]{0,1:T(8,128)(2,1)} fusion(f32[16,4096]{0,1:T(8,128)S(1)} %copy.31, f32[32]{0:T(128)S(1)} %iota_negate_fusion, f32[16,4096]{0,1:T(8,128)} %copy.30), kind=kLoop, calls=%fused_computation.12 | loop fusion | flops 6160384 | bytes 786560 | tf_op jit(solution)/shard_map/reduce_sum | solution.py:32
  107.5 1.5 copy.32
  109.1 5.6 %fusion.20 = bf16[4096,32,32]{0,2,1:T(8,128)(2,1)} fusion(s32[32,32]{1,0:T(8,128)S(1)} %iota_subtract_fusion, bf16[32,4096]{1,0:T(8,128)(2,1)S(1)} %copy.32), kind=kOutput, calls=%fused_computation.26 | convolution fusion | flops 268468224 | bytes 8654848 | tf_op jit(solution)/shard_map/dot_general | solution.py:42
  114.7 44.1 %copy.33 = bf16[4096,32,32]{2,1,0:T(8,128)(2,1)} copy(bf16[4096,32,32]{0,2,1:T(8,128)(2,1)} %fusion.20) | data formatting | bytes 16777216 | tf_op jit(solution)/shard_map/dot_general | solution.py:42
  158.9 22.7 %fusion.24 = f32[4096,32,4]{1,2,0:T(4,128)} fusion(bf16[4096,32,32]{2,1,0:T(8,128)(2,1)} %copy.33, bf16[4,32,4096]{1,0,2:T(4,128)(2,1)} %copy.34), kind=kOutput, calls=%fused_computation.38 | convolution fusion | flops 33554432 | bytes 11534336 | tf_op jit(solution)/shard_map/dts,nsd->ntd/dot_general | solution.py:46
  181.6 143.5 %all-gather.7.cloned.1.call-done = f32[512,4096]{1,0:T(8,128)} async-done(((f32[16,4096]{1,0:T(8,128)}), f32[512,4096]{1,0:T(8,128)}) %all-gather.7.cloned.1.call-update) | async-done | bytes 8388624 | tf_op jit(solution)/shard_map/all_gather | solution.py:12
  325.1 39.4 %while.28 = (s32[]{:T(128)}, f32[16,4096]{1,0:T(8,128)S(1)}, s32[]{:T(128)}, f32[32,16,4096]{2,1,0:T(8,128)}, f32[32,16,4096]{2,1,0:T(8,128)}, /*index=5*/s32[]{:T(128)}, s32[]{:T(128)}) while((s32[]{:T(128)}, f32[16,4096]{1,0:T(8,128)S(1)}, s32[]{:T(128)}, f32[32,16,4096]{2,1,0:T(8,128)}, f32[32,16,4096]{2,1,0:T(8,128)}, ...), condition=%wide.region_4.5_spmd.clone, body=%wide.region_3.4_spmd.clone.sunk | while | flops 262148 | bytes 1048685 | solution.py:21
  331.4 1.2 fusion.35
  364.5 2.5 multiply_add_fusion
  367.0 6.9 %copy.37 = f32[4,16,4096]{1,0,2:T(4,128)} copy(f32[4,16,4096]{2,1,0:T(8,128)} %multiply_add_fusion) | data formatting | bytes 2097152 | tf_op jit(solution)/shard_map/add | solution.py:68
  374.0 47.3 %bitcast_add_fusion.2 = f32[4,32,4096]{1,0,2:T(4,128)} fusion(f32[4096,32,4]{1,2,0:T(4,128)} %fusion.24, f32[4,16,4096]{1,0,2:T(4,128)} %copy.37, f32[32]{0:T(128)S(1)} %add_negate_fusion, f32[16,4096]{0,1:T(8,128)S(1)} %copy.31, f32[16,4096]{0,1:T(8,128)} %copy.30), kind=kOutput, calls=%fused_computation.18 | convolution fusion | flops 105381888 | bytes 5767296 | tf_op jit(solution)/shard_map/tkd,nkd->ntd/dot_general | solution.py:72
  421.3 7.0 %copy.38 = f32[4,32,4096]{2,1,0:T(8,128)S(1)} copy(f32[4,32,4096]{1,0,2:T(4,128)} %bitcast_add_fusion.2) | data formatting | bytes 4194304 | tf_op jit(solution)/shard_map/add | solution.py:73
  428.3 2.1 fusion.19
  430.3 62.8 %all-to-all-done = bf16[32,128,2048]{2,1,0:T(8,128)(2,1)} async-done(((bf16[32,128,2048]{2,1,0:T(8,128)(2,1)}), bf16[32,128,2048]{2,1,0:T(8,128)(2,1)}, u32[]{:S(2)}, u32[]{:S(2)}) %all-to-all-start) | async-done | bytes 16777248 | tf_op jit(solution)/shard_map/all_to_all | solution.py:78
  493.1 8.9 %convolution_convert_fusion = bf16[128,2048]{1,0:T(8,128)(2,1)} fusion(bf16[128,4096]{1,0:T(8,128)(2,1)S(1)} %fusion.19, bf16[4096,2048]{1,0:T(8,128)(2,1)} %bitcast.10), kind=kOutput, calls=%fused_computation.20 | convolution fusion | flops 2147745792 | bytes 18350080 | tf_op jit(solution)/shard_map/dot_general | solution.py:80
  (59 shorter events, 45.7 us)
Async XLA Ops:
  6.5 175.0 %all-gather.5.cloned.1.call-start = ((), (), s32[]{:S(2)}) async-start(), calls=%async_computation.1 | async-start | bytes 8650752 | tf_op jit(solution)/shard_map/all_gather | solution.py:12
  8.5 316.6 %all-gather.7.cloned.1.call-start = ((), (), s32[]{:S(2)}) async-start(), calls=%async_computation.2 | async-start | bytes 8650752 | tf_op jit(solution)/shard_map/all_gather | solution.py:12
  50.4 15.8 %copy-start.2 = (bf16[128,2048]{1,0:T(8,128)(2,1)S(1)}, bf16[128,2048]{1,0:T(8,128)(2,1)}, u32[]{:S(2)}) copy-start(bf16[128,2048]{1,0:T(8,128)(2,1)} %param.15) | copy-start | bytes 1572868
  65.5 0.7 copy-start
  72.3 420.8 %all-to-all-start = ((bf16[32,128,2048]{2,1,0:T(8,128)(2,1)}), bf16[32,128,2048]{2,1,0:T(8,128)(2,1)}, u32[]{:S(2)}, u32[]{:S(2)}) async-start(bf16[32,128,2048]{2,1,0:T(8,128)(2,1)} %stack.2), calls=%async_computation | async-start | bytes 33554432 | tf_op jit(solution)/shard_map/all_to_all | solution.py:78
  158.8 205.6 %copy-start.1 = (f32[4096,16]{0,1:T(8,128)S(1)}, f32[4096,16]{0,1:T(8,128)}, u32[]{:S(2)}) copy-start(f32[4096,16]{0,1:T(8,128)} %param.12) | copy-start | bytes 786436
  421.3 7.0 %copy-start.3 = (f32[4096]{0:T(1024)S(1)}, f32[4096]{0:T(1024)}, u32[]{:S(2)}) copy-start(f32[4096]{0:T(1024)} %param.14) | copy-start | bytes 49156
Sparse Core Ops, SparseCore 0:
  10.2 82.8 all-gather.4
  96.0 229.0 all-gather.6
